TPU v7x, 32 devices: a whole 2x2x4 slice. The times are simulated.
32 devices in a mesh: tint: 8 (over z, x), tsec: 4 (over y, core).
Axes of the slice: x: 2, y: 2, z: 4, core: 2. Of those that a mesh axis runs over, the one named last changes fastest.
Arguments:
- history: bfloat16 [16, 2, 128, 16, 128], P('tint', None, None, 'tsec'), may hold values from -6 to 6
- first_row: float32 [2, 128, 16, 128], P(None, None, 'tsec'), may hold values from -6 to 6
- hamiltonian: float32 [128, 128], replicated, may hold values from -0.5 to 0.5
- coupling: float32 [128, 128], replicated, may hold values from 0.001 to 0.01
- window_start: int32 [128], replicated, may hold values from 0 to 7
- block_time: int32 [8], P('tint'), may hold values from 0 to 7, each once
Outputs:
- last_row: float32 [2, 128, 16, 128], P(None, None, 'tsec')
Inputs may be any that keep to these rules, and one draw needn't show every extreme that they name: `block_time`: each block number appears once.
All inputs are finite; a program needn't handle non-finite values.
Results may differ from a plain program's by a relative error of at most 0.0058.
Values may be sent and summed in bfloat16 or wider, within the bound.
No kernel may reach another device: no remote copies, remote signals or barrier semaphores. Data moves between devices by JAX's collectives and lax.ppermute only.
A program may use at most 64 MiB of HBM per device.

v0:
```python
import jax
import jax.numpy as jnp
from jax import lax
from jax.sharding import PartitionSpec as P


def from_root(x, axis, root):
    mine = lax.axis_index(axis) == root
    return lax.psum(jnp.where(mine, x, jnp.zeros_like(x)), axis)


def shards(history, first_row, hamiltonian, coupling, window_start, block_time):
    points = history.shape[0]
    orbital_count = history.shape[2]
    second_time = history.shape[3]
    first = block_time[0] * points
    root = first // second_time
    offset = first % second_time
    times = first + jnp.arange(points, dtype=jnp.int32)
    live = (times[None, :] >= window_start[:, None]).astype(jnp.float32)
    history_window_real = history[:, 0].reshape(points * orbital_count, second_time * orbital_count)
    history_window_imag = history[:, 1].reshape(points * orbital_count, second_time * orbital_count)
    rounded = first_row.astype(jnp.bfloat16)
    piece = lax.dynamic_slice_in_dim(rounded, offset, points, 2)
    owned = from_root(piece, "tsec", root).astype(jnp.float32)
    real_part = owned[0]
    imag_part = owned[1]
    factor = (
        -coupling[:, None, :] * live[:, :, None] * (real_part * real_part + imag_part * imag_part)
    )
    self_energy_real = (
        (factor * real_part).astype(jnp.bfloat16).reshape(orbital_count, points * orbital_count)
    )
    self_energy_imag = (
        (factor * imag_part).astype(jnp.bfloat16).reshape(orbital_count, points * orbital_count)
    )
    collision_integral_real = jnp.dot(
        self_energy_real, history_window_real, preferred_element_type=jnp.float32
    ) - jnp.dot(self_energy_imag, history_window_imag, preferred_element_type=jnp.float32)
    collision_integral_imag = jnp.dot(
        self_energy_real, history_window_imag, preferred_element_type=jnp.float32
    ) + jnp.dot(self_energy_imag, history_window_real, preferred_element_type=jnp.float32)
    partial_collision_terms = jnp.stack([collision_integral_real, collision_integral_imag]).reshape(
        2, orbital_count, second_time, orbital_count
    )
    flattened_real = first_row[0].reshape(orbital_count, second_time * orbital_count)
    flattened_imag = first_row[1].reshape(orbital_count, second_time * orbital_count)
    summed = lax.psum(partial_collision_terms, "tint")
    hamiltonian_green_real = jnp.dot(hamiltonian, flattened_real, precision=lax.Precision.HIGHEST)
    hamiltonian_green_imag = jnp.dot(hamiltonian, flattened_imag, precision=lax.Precision.HIGHEST)
    advanced_real = flattened_real + 0.25 * (
        hamiltonian_green_imag + summed[1].reshape(orbital_count, second_time * orbital_count)
    )
    advanced_imag = flattened_imag - 0.25 * (
        hamiltonian_green_real + summed[0].reshape(orbital_count, second_time * orbital_count)
    )
    updated = jnp.stack([advanced_real, advanced_imag]).reshape(
        2, orbital_count, second_time, orbital_count
    )
    return updated


def solution(mesh):
    return jax.shard_map(
        shards,
        mesh=mesh,
        in_specs=(
            P("tint", None, None, "tsec", None),
            P(None, None, "tsec", None),
            P(),
            P(),
            P(),
            P("tint"),
        ),
        out_specs=P(None, None, "tsec", None),
        check_vma=False,
    )
```

profile of v0, /device:TPU:0, one launch (start us, length us, event | category | flops | bytes accessed | tf_op | source)
XLA Modules:
  0.0 130.2 jit_solution(7736346119339455793)
XLA Ops:
  7.3 1.2 constant_dynamic-slice_fusion
  8.5 0.1 copy.9
  8.6 0.7 convert_select_fusion
  9.4 0.2 fusion.20
  9.6 0.4 copy-done.4
  10.1 0.1 copy-done.3
  10.2 0.1 copy.7
  10.3 33.9 %all-reduce.3.cloned.1.call-done = bf16[2,128,2,128]{1,3,2,0:T(8,128)(2,1)} async-done(((bf16[2,128,2,128]{1,3,2,0:T(8,128)(2,1)}), bf16[2,128,2,128]{1,3,2,0:T(8,128)(2,1)}) %all-reduce.3.cloned.1.call-update) | async-done | bytes 131088 | tf_op jit(solution)/shard_map/psum | solution.py:9
  44.2 0.9 convert_element_type.31
  45.2 0.2 fusion.4
  45.4 0.2 fusion.8
  45.6 0.2 convolution_add_fusion.1
  45.8 0.2 convolution_subtract_fusion
  46.0 0.1 stack.18
  46.1 0.1 stack.19
  46.2 0.9 pad_maximum_fusion
  47.2 1.0 copy-done.1
  48.2 72.2 %all-reduce.5.cloned.1.call-done = f32[2,128,4,128]{3,2,1,0:T(4,128)} async-done(((f32[2,128,4,128]{3,2,1,0:T(4,128)}), f32[2,128,4,128]{3,2,1,0:T(4,128)}) %all-reduce.5.cloned.1.call-update) | async-done | bytes 524304 | tf_op jit(solution)/shard_map/psum | solution.py:48
  120.4 1.1 fusion.18
  121.5 0.4 fusion.1
  121.9 0.4 fusion.3
  122.3 0.1 stack.21
  122.4 0.1 stack.22
  122.5 0.9 pad_maximum_fusion.1
  (16 shorter events, 0.3 us)
Async XLA Ops:
  6.5 115.0 %copy-start = (f32[128,128]{1,0:T(8,128)S(1)}, f32[128,128]{1,0:T(8,128)}, u32[]{:S(2)}) copy-start(f32[128,128]{1,0:T(8,128)} %param.8) | copy-start | bytes 196612
  6.5 2.8 %copy-start.2 = (bf16[2,2,128,4,128]{4,3,2,1,0:T(4,128)(2,1)S(1)}, bf16[2,2,128,4,128]{4,3,2,1,0:T(4,128)(2,1)}, u32[]{:S(2)}) copy-start(bf16[2,2,128,4,128]{4,3,2,1,0:T(4,128)(2,1)} %param.6) | copy-start | bytes 1572868
  6.5 37.7 %all-reduce.3.cloned.1.call-start = ((), (), s32[]{:S(2)}) async-start(), calls=%async_computation | async-start | bytes 262144 | tf_op jit(solution)/shard_map/psum | solution.py:9
  9.3 111.1 %all-reduce.5.cloned.1.call-start = ((), (), s32[]{:S(2)}) async-start(), calls=%async_computation.1 | async-start | bytes 1048576 | tf_op jit(solution)/shard_map/psum | solution.py:48
  9.4 0.7 copy-start.4
  9.4 0.8 copy-start.3
  47.1 1.0 copy-start.1
Sparse Core Ops, SparseCore 0:
  9.6 34.4 all-reduce.2
  47.6 72.7 all-reduce.4
where the time goes:
time: 131 us; the launch traced here: 130 us
  waiting for transfers between devices  106 us (81%)
  between operations  14.3 us (11%)
  local copies, waits for them, and re-layouts  4.64 us (4%)
  other arithmetic  3.55 us (3%)
  matrix products  1.6 us (1%)
    psum x1, waiting for transfers between devices, shards(): summed = lax.psum(partial_collision_terms, 'tint')  72.2 us
    psum x1, waiting for transfers between devices, from_root(): return lax.psum(jnp.where(mine, x, jnp.zeros_like(x)), axis)  33.9 us
  transfers between devices with their start and end apart: 2, of which 2 were waited for; matrix products, arithmetic and copies ran while one was open for 0% of the time, Pallas kernels for 0%

commit v1 on v0

v1 whole, which is shorter than its diff:
```python
import math

import jax
import jax.numpy as jnp
from jax import lax
from jax.sharding import PartitionSpec as P


def from_root(x, axis, size, root):
    me = lax.axis_index(axis)
    bit = 1
    if size & (size - 1) == 0:
        while bit < size:
            other = lax.ppermute(x, axis, [(i, i ^ bit) for i in range(size)])
            x = jnp.where((root & bit) == (me & bit), x, other)
            bit *= 2
        return x
    mine = x
    for k in range(1, size):
        got = lax.ppermute(mine, axis, [(i, (i + k) % size) for i in range(size)])
        x = jnp.where((root + k) % size == me, got, x)
    return x


def shift_outer(x, axis, outer, inner, k):
    pairs = [
        (o * inner + n, (o + k) % outer * inner + n) for o in range(outer) for n in range(inner)
    ]
    return lax.ppermute(x, axis, pairs)


def shift_inner(x, axis, outer, inner, k):
    pairs = [
        (o * inner + n, o * inner + (n + k) % inner) for o in range(outer) for n in range(inner)
    ]
    return lax.ppermute(x, axis, pairs)


def sum_over(parts, axis, outer, inner):
    place = lax.axis_index(axis) // inner
    sent = parts.astype(jnp.bfloat16)
    total = lax.dynamic_index_in_dim(parts, place, 0, keepdims=False)
    order = sorted(range(1, outer), key=lambda k: -min(k, outer - k))
    for k in order:
        chunk = lax.dynamic_index_in_dim(sent, (place + k) % outer, 0, keepdims=False)
        total = total + shift_outer(chunk, axis, outer, inner, k).astype(jnp.float32)
    mine = total.astype(jnp.bfloat16)
    position = lax.axis_index(axis) % inner
    pieces = [mine] + [shift_inner(mine, axis, outer, inner, k) for k in range(1, inner)]
    if inner == 2:
        mine = (pieces[0].astype(jnp.float32) + pieces[1].astype(jnp.float32)).astype(jnp.bfloat16)
    else:
        ordered = jnp.stack(pieces)
        mine = sum(
            lax.dynamic_index_in_dim(ordered, (position - n) % inner, 0, keepdims=False).astype(
                jnp.float32
            )
            for n in range(inner)
        ).astype(jnp.bfloat16)
    gathered = {0: mine}
    for k in order:
        gathered[k] = shift_outer(mine, axis, outer, inner, k)
    ordered = jnp.stack([gathered[k] for k in range(outer)])
    return jnp.stack(
        [
            lax.dynamic_index_in_dim(ordered, (place - q) % outer, 0, keepdims=False)
            for q in range(outer)
        ]
    )


def shards(tint_size, tsec_size, history, first_row, hamiltonian, coupling, window_start, block_time):
    points, _, orbitals, second_time, _ = history.shape
    first = block_time[0] * points
    root = first // second_time
    offset = first % second_time
    times = first + jnp.arange(points, dtype=jnp.int32)
    live = (times[None, :] >= window_start[:, None]).astype(jnp.float32)
    piece = lax.dynamic_slice_in_dim(first_row, offset, points, 2).astype(jnp.bfloat16)
    owned = from_root(piece, "tsec", tsec_size, root).astype(jnp.float32)
    real_part, imag_part = owned[0], owned[1]
    factor = (
        -coupling[:, None, :] * live[:, :, None] * (real_part * real_part + imag_part * imag_part)
    )
    sr = (factor * real_part).astype(jnp.bfloat16)
    si = (factor * imag_part).astype(jnp.bfloat16)
    left = jnp.stack([jnp.stack([sr, -si], 2), jnp.stack([si, sr], 2)])
    left = left.reshape(2 * orbitals, points * 2 * orbitals)
    window = history.reshape(points * 2 * orbitals, second_time * orbitals)
    terms = jnp.dot(left, window, preferred_element_type=jnp.float32)
    inner = max(d for d in range(1, math.isqrt(tint_size) + 1) if tint_size % d == 0)
    outer = tint_size // inner
    parts = terms.reshape(2, outer, orbitals // outer, second_time * orbitals).swapaxes(0, 1)
    summed = sum_over(parts, "tint", outer, inner)
    summed = summed.swapaxes(0, 1).reshape(2, orbitals, second_time * orbitals).astype(jnp.float32)
    flat = first_row.reshape(2, orbitals, second_time * orbitals)
    hg_real = jnp.dot(hamiltonian, flat[0], precision=lax.Precision.HIGHEST)
    hg_imag = jnp.dot(hamiltonian, flat[1], precision=lax.Precision.HIGHEST)
    advanced_real = flat[0] + 0.25 * (hg_imag + summed[1])
    advanced_imag = flat[1] - 0.25 * (hg_real + summed[0])
    return jnp.stack([advanced_real, advanced_imag]).reshape(first_row.shape)


def solution(mesh):
    tint_size, tsec_size = mesh.shape["tint"], mesh.shape["tsec"]

    def step(*arrays):
        return shards(tint_size, tsec_size, *arrays)

    return jax.shard_map(
        step,
        mesh=mesh,
        in_specs=(
            P("tint", None, None, "tsec", None),
            P(None, None, "tsec", None),
            P(),
            P(),
            P(),
            P("tint"),
        ),
        out_specs=P(None, None, "tsec", None),
        check_vma=False,
    )
```

time: 131 us -> 38.3 us (0.29)
  waiting for transfers between devices: 106 us -> 18.2 us
  between operations: 14.3 us -> 1.03 us
  starting transfers between devices: 0.04 us -> 12.2 us
  other arithmetic: 3.55 us -> 2.17 us
    psum x2 -> x0, waiting for transfers between devices: 106 us -> none  [the longest x1 72.2 us: shards(): summed = lax.psum(partial_collision_terms, 'tint')]
    ppermute x0 -> x9, waiting for transfers between devices: none -> 18.2 us  [the longest x6 11.6 us: shift_outer(): return lax.ppermute(x, axis, pairs)]
    ppermute x0 -> x9, starting transfers between devices: none -> 12.2 us  [the longest x6 7.41 us: shift_outer(): return lax.ppermute(x, axis, pairs)]
    unnamed x11 -> x8, local copies, waits for them, and re-layouts: 1.73 us -> 0.02 us
  transfers between devices with their start and end apart: 2 -> 9, of which waited for: 2 -> 7; matrix products, arithmetic and copies ran while one was open for 0% -> 4% of each run, Pallas kernels for 0% -> 0%
where the time goes in v1:
time: 38.3 us; the launch traced here: 38.1 us
  waiting for transfers between devices  18.2 us (48%)
  starting transfers between devices  12.2 us (32%)
  local copies, waits for them, and re-layouts  3.43 us (9%)
  other arithmetic  2.17 us (6%)
  matrix products  1.06 us (3%)
  between operations  1.03 us (3%)
    ppermute x6, waiting for transfers between devices, shift_outer(): return lax.ppermute(x, axis, pairs)  11.6 us
    ppermute x6, starting transfers between devices, shift_outer(): return lax.ppermute(x, axis, pairs)  7.41 us
    ppermute x2, waiting for transfers between devices, from_root(): other = lax.ppermute(x, axis, [(i, i ^ bit) for i in range(size)])  3.83 us
    ppermute x2, starting transfers between devices, from_root(): other = lax.ppermute(x, axis, [(i, i ^ bit) for i in range(size)])  3.24 us
    ppermute x1, waiting for transfers between devices, shift_inner(): return lax.ppermute(x, axis, pairs)  2.77 us
    ppermute x1, starting transfers between devices, shift_inner(): return lax.ppermute(x, axis, pairs)  1.56 us
    reshape x1, local copies, waits for them, and re-layouts, shards(): window = history.reshape(points * 2 * orbitals, second_time * orbitals)  1.3 us
    convert_element_type x1, local copies, waits for them, and re-layouts, shards(): lax.dynamic_slice_in_dim(first_row, offset, points, 2).astype(jnp.bfloat16)  1.17 us
  transfers between devices with their start and end apart: 9, of which 7 were waited for; matrix products, arithmetic and copies ran while one was open for 4% of the time, Pallas kernels for 0%

profile of v1, /device:TPU:0, one launch (start us, length us, event | category | flops | bytes accessed | tf_op | source)
XLA Modules:
  0.0 38.1 jit_solution(15915910723520614959)
XLA Ops:
  0.7 1.2 %dynamic-slice_convert_fusion = bf16[2,128,2,128]{3,2,1,0:T(2,128)(2,1)S(1)} fusion(f32[2,128,4,128]{3,2,1,0:T(4,128)} %param.7, s32[]{:T(128)S(6)} %select_n.89), kind=kLoop, calls=%fused_computation.16 | loop fusion | bytes 262148 | tf_op jit(solution)/shard_map/convert_element_type | solution.py:79
  1.9 0.6 %collective-permute-start = (bf16[2,128,2,128]{3,2,1,0:T(2,128)(2,1)S(1)}, bf16[2,128,2,128]{3,2,1,0:T(2,128)(2,1)S(1)}, u32[]{:S(2)}, u32[]{:S(2)}) collective-permute-start(bf16[2,128,2,128]{3,2,1,0:T(2,128)(2,1)S(1)} %dynamic-slice_convert_fusion), channel_id=1, source_target_pairs={{0,1},{1,0},{2,3},{3,2},{4,5},{5,4},{6,7},{7,6},{8,9},{9,8},{10,11... | collective-permute-start | bytes 393224 | tf_op jit(solution)/shard_map/ppermute | solution.py:14
  2.4 1.3 %reshape.148 = bf16[512,512,1,1]{1,0,2,3:T(8,128)(2,1)S(1)} reshape(bf16[2,2,128,4,128]{4,3,2,1,0:T(4,128)(2,1)} %param.6) | data formatting | bytes 1048576 | tf_op jit(solution)/shard_map/reshape | solution.py:89
  4.0 2.7 %collective-permute-start.1 = (bf16[2,128,2,128]{3,2,1,0:T(2,128)(2,1)S(1)}, bf16[2,128,2,128]{3,2,1,0:T(2,128)(2,1)S(1)}, u32[]{:S(2)}, u32[]{:S(2)}) collective-permute-start(bf16[2,128,2,128]{3,2,1,0:T(2,128)(2,1)S(1)} %broadcast_select_fusion), channel_id=1, source_target_pairs={{0,2},{1,3},{2,0},{3,1},{4,6},{5,7},{6,4},{7,5},{8,10},{9,11},{10,... | collective-permute-start | bytes 393224 | tf_op jit(solution)/shard_map/ppermute | solution.py:14
  6.9 3.8 %collective-permute-done.1 = bf16[2,128,2,128]{3,2,1,0:T(2,128)(2,1)S(1)} collective-permute-done((bf16[2,128,2,128]{3,2,1,0:T(2,128)(2,1)S(1)}, bf16[2,128,2,128]{3,2,1,0:T(2,128)(2,1)S(1)}, u32[]{:S(2)}, u32[]{:S(2)}) %collective-permute-start.1) | collective-permute-done | bytes 131104 | tf_op jit(solution)/shard_map/ppermute | solution.py:14
  10.9 0.2 fusion.18
  11.1 0.2 multiply_convert_fusion.1
  11.3 0.3 pad_maximum_fusion.2
  11.6 0.2 copy.14
  12.2 0.3 fusion.21
  12.5 3.9 %collective-permute-start.4 = (bf16[2,32,512]{2,1,0:T(8,128)(2,1)S(1)}, bf16[2,32,512]{2,1,0:T(8,128)(2,1)S(1)}, u32[]{:S(2)}, u32[]{:S(2)}) collective-permute-start(bf16[2,32,512]{2,1,0:T(8,128)(2,1)S(1)} %get-tuple-element.16), channel_id=1, source_target_pairs={{0,24},{4,28},{8,0},{12,4},{16,8},{20,12},{24,16},{28,20},{1,25},{... | collective-permute-start | bytes 196616 | tf_op jit(solution)/shard_map/ppermute | solution.py:29
  16.4 1.0 %collective-permute-start.2 = (bf16[2,32,512]{2,1,0:T(8,128)(2,1)S(1)}, bf16[2,32,512]{2,1,0:T(8,128)(2,1)S(1)}, u32[]{:S(2)}, u32[]{:S(2)}) collective-permute-start(bf16[2,32,512]{2,1,0:T(8,128)(2,1)S(1)} %get-tuple-element.15), channel_id=1, source_target_pairs={{0,16},{4,20},{8,24},{12,28},{16,0},{20,4},{24,8},{28,12},{1,17},{... | collective-permute-start | bytes 196616 | tf_op jit(solution)/shard_map/ppermute | solution.py:29
  17.4 1.5 %collective-permute-done.4 = bf16[2,32,512]{2,1,0:T(8,128)(2,1)S(1)} collective-permute-done((bf16[2,32,512]{2,1,0:T(8,128)(2,1)S(1)}, bf16[2,32,512]{2,1,0:T(8,128)(2,1)S(1)}, u32[]{:S(2)}, u32[]{:S(2)}) %collective-permute-start.4) | collective-permute-done | bytes 65568 | tf_op jit(solution)/shard_map/ppermute | solution.py:29
  18.9 3.6 %collective-permute-done.3 = bf16[2,32,512]{2,1,0:T(8,128)(2,1)S(1)} collective-permute-done((bf16[2,32,512]{2,1,0:T(8,128)(2,1)S(1)}, bf16[2,32,512]{2,1,0:T(8,128)(2,1)S(1)}, u32[]{:S(2)}, u32[]{:S(2)}) %collective-permute-start.3) | collective-permute-done | bytes 65568 | tf_op jit(solution)/shard_map/ppermute | solution.py:29
  22.4 1.1 %collective-permute-done.2 = bf16[2,32,512]{2,1,0:T(8,128)(2,1)S(1)} collective-permute-done((bf16[2,32,512]{2,1,0:T(8,128)(2,1)S(1)}, bf16[2,32,512]{2,1,0:T(8,128)(2,1)S(1)}, u32[]{:S(2)}, u32[]{:S(2)}) %collective-permute-start.2) | collective-permute-done | bytes 65568 | tf_op jit(solution)/shard_map/ppermute | solution.py:29
  23.6 1.6 %collective-permute-start.5 = (bf16[2,32,512]{2,1,0:T(8,128)(2,1)S(1)}, bf16[2,32,512]{2,1,0:T(8,128)(2,1)S(1)}, u32[]{:S(2)}, u32[]{:S(2)}) collective-permute-start(bf16[2,32,512]{2,1,0:T(8,128)(2,1)S(1)} %fusion.16), channel_id=1, source_target_pairs={{0,4},{4,0},{8,12},{12,8},{16,20},{20,16},{24,28},{28,24},{1,5},{5... | collective-permute-start | bytes 196616 | tf_op jit(solution)/shard_map/ppermute | solution.py:36
  25.1 2.8 %collective-permute-done.5 = bf16[2,32,512]{2,1,0:T(8,128)(2,1)S(1)} collective-permute-done((bf16[2,32,512]{2,1,0:T(8,128)(2,1)S(1)}, bf16[2,32,512]{2,1,0:T(8,128)(2,1)S(1)}, u32[]{:S(2)}, u32[]{:S(2)}) %collective-permute-start.5) | collective-permute-done | bytes 65568 | tf_op jit(solution)/shard_map/ppermute | solution.py:36
  27.9 1.9 %collective-permute-start.8 = (bf16[2,32,512]{2,1,0:T(8,128)(2,1)S(1)}, bf16[2,32,512]{2,1,0:T(8,128)(2,1)S(1)}, u32[]{:S(2)}, u32[]{:S(2)}) collective-permute-start(bf16[2,32,512]{2,1,0:T(8,128)(2,1)S(1)} %add_convert_fusion), channel_id=1, source_target_pairs={{0,24},{4,28},{8,0},{12,4},{16,8},{20,12},{24,16},{28,20},{1,25},{... | collective-permute-start | bytes 196616 | tf_op jit(solution)/shard_map/ppermute | solution.py:29
  29.8 0.6 %collective-permute-start.6 = (bf16[2,32,512]{2,1,0:T(8,128)(2,1)S(1)}, bf16[2,32,512]{2,1,0:T(8,128)(2,1)S(1)}, u32[]{:S(2)}, u32[]{:S(2)}) collective-permute-start(bf16[2,32,512]{2,1,0:T(8,128)(2,1)S(1)} %add_convert_fusion), channel_id=1, source_target_pairs={{0,8},{4,12},{8,16},{12,20},{16,24},{20,28},{24,0},{28,4},{1,9},{5... | collective-permute-start | bytes 196616 | tf_op jit(solution)/shard_map/ppermute | solution.py:29
  30.6 2.0 %collective-permute-done.8 = bf16[2,32,512]{2,1,0:T(8,128)(2,1)S(1)} collective-permute-done((bf16[2,32,512]{2,1,0:T(8,128)(2,1)S(1)}, bf16[2,32,512]{2,1,0:T(8,128)(2,1)S(1)}, u32[]{:S(2)}, u32[]{:S(2)}) %collective-permute-start.8) | collective-permute-done | bytes 65568 | tf_op jit(solution)/shard_map/ppermute | solution.py:29
  32.5 3.5 %collective-permute-done.7 = bf16[2,32,512]{2,1,0:T(8,128)(2,1)S(1)} collective-permute-done((bf16[2,32,512]{2,1,0:T(8,128)(2,1)S(1)}, bf16[2,32,512]{2,1,0:T(8,128)(2,1)S(1)}, u32[]{:S(2)}, u32[]{:S(2)}) %collective-permute-start.7) | collective-permute-done | bytes 65568 | tf_op jit(solution)/shard_map/ppermute | solution.py:29
  36.2 0.4 %fusion.1 = f32[128,512]{1,0:T(8,128)S(1)} fusion(f32[128,512]{1,0:T(8,128)S(1)} %bitcast.67, f32[128,128]{1,0:T(8,128)S(1)} %copy-done, f32[16,8,4,128]{3,2,1,0:T(4,128)S(1)} %bitcast.64, f32[16,8,4,128]{3,2,1,0:T(4,128)S(1)} %bitcast.62), kind=kOutput, calls=%fused_computation.2 | convolution fusion | flops 100859904 | bytes 1114112 | tf_op jit(solution)/shard_map/dot_general | solution.py:97
  36.7 0.4 fusion.3
  37.2 0.9 %pad_maximum_fusion = f32[2,128,4,128]{3,2,1,0:T(4,128)} fusion(f32[1,128,4,128]{3,2,1,0:T(4,128)S(1)} %stack.62, f32[1,128,4,128]{3,2,1,0:T(4,128)S(1)} %stack.61), kind=kLoop, calls=%fused_computation.6 | loop fusion | flops 131072 | bytes 1048576 | tf_op jit(solution)/shard_map/stack | solution.py:101
  (31 shorter events, 1.3 us)
Async XLA Ops:
  0.0 36.2 %copy-start = (f32[128,128]{1,0:T(8,128)S(1)}, f32[128,128]{1,0:T(8,128)}, u32[]{:S(2)}) copy-start(f32[128,128]{1,0:T(8,128)} %param.8) | copy-start | bytes 196612
  1.9 1.9 %collective-permute-start = (bf16[2,128,2,128]{3,2,1,0:T(2,128)(2,1)S(1)}, bf16[2,128,2,128]{3,2,1,0:T(2,128)(2,1)S(1)}, u32[]{:S(2)}, u32[]{:S(2)}) collective-permute-start(bf16[2,128,2,128]{3,2,1,0:T(2,128)(2,1)S(1)} %dynamic-slice_convert_fusion), channel_id=1, source_target_pairs={{0,1},{1,0},{2,3},{3,2},{4,5},{5,4},{6,7},{7,6},{8,9},{9,8},{10,11... | collective-permute-start | bytes 393224 | tf_op jit(solution)/shard_map/ppermute | solution.py:14
  2.4 1.3 %copy-start.1 = (f32[2,128,4,128]{3,2,1,0:T(4,128)S(1)}, f32[2,128,4,128]{3,2,1,0:T(4,128)}, u32[]{:S(2)}) copy-start(f32[2,128,4,128]{3,2,1,0:T(4,128)} %param.7) | copy-start | bytes 1572868
  3.8 2.9 %copy-start.3 = (s32[128]{0:T(128)S(1)}, s32[128]{0:T(128)}, u32[]{:S(2)}) copy-start(s32[128]{0:T(128)} %param.10) | copy-start | bytes 1540
  4.0 2.9 %copy-start.2 = (f32[128,128]{1,0:T(8,128)S(1)}, f32[128,128]{1,0:T(8,128)}, u32[]{:S(2)}) copy-start(f32[128,128]{1,0:T(8,128)} %param.9) | copy-start | bytes 196612
  4.0 6.7 %collective-permute-start.1 = (bf16[2,128,2,128]{3,2,1,0:T(2,128)(2,1)S(1)}, bf16[2,128,2,128]{3,2,1,0:T(2,128)(2,1)S(1)}, u32[]{:S(2)}, u32[]{:S(2)}) collective-permute-start(bf16[2,128,2,128]{3,2,1,0:T(2,128)(2,1)S(1)} %broadcast_select_fusion), channel_id=1, source_target_pairs={{0,2},{1,3},{2,0},{3,1},{4,6},{5,7},{6,4},{7,5},{8,10},{9,11},{10,... | collective-permute-start | bytes 393224 | tf_op jit(solution)/shard_map/ppermute | solution.py:14
  12.5 6.4 %collective-permute-start.4 = (bf16[2,32,512]{2,1,0:T(8,128)(2,1)S(1)}, bf16[2,32,512]{2,1,0:T(8,128)(2,1)S(1)}, u32[]{:S(2)}, u32[]{:S(2)}) collective-permute-start(bf16[2,32,512]{2,1,0:T(8,128)(2,1)S(1)} %get-tuple-element.16), channel_id=1, source_target_pairs={{0,24},{4,28},{8,0},{12,4},{16,8},{20,12},{24,16},{28,20},{1,25},{... | collective-permute-start | bytes 196616 | tf_op jit(solution)/shard_map/ppermute | solution.py:29
  16.4 6.1 %collective-permute-start.3 = (bf16[2,32,512]{2,1,0:T(8,128)(2,1)S(1)}, bf16[2,32,512]{2,1,0:T(8,128)(2,1)S(1)}, u32[]{:S(2)}, u32[]{:S(2)}) collective-permute-start(bf16[2,32,512]{2,1,0:T(8,128)(2,1)S(1)} %get-tuple-element.17), channel_id=1, source_target_pairs={{0,8},{4,12},{8,16},{12,20},{16,24},{20,28},{24,0},{28,4},{1,9},{5... | collective-permute-start | bytes 196616 | tf_op jit(solution)/shard_map/ppermute | solution.py:29
  16.4 7.2 %collective-permute-start.2 = (bf16[2,32,512]{2,1,0:T(8,128)(2,1)S(1)}, bf16[2,32,512]{2,1,0:T(8,128)(2,1)S(1)}, u32[]{:S(2)}, u32[]{:S(2)}) collective-permute-start(bf16[2,32,512]{2,1,0:T(8,128)(2,1)S(1)} %get-tuple-element.15), channel_id=1, source_target_pairs={{0,16},{4,20},{8,24},{12,28},{16,0},{20,4},{24,8},{28,12},{1,17},{... | collective-permute-start | bytes 196616 | tf_op jit(solution)/shard_map/ppermute | solution.py:29
  23.6 4.3 %collective-permute-start.5 = (bf16[2,32,512]{2,1,0:T(8,128)(2,1)S(1)}, bf16[2,32,512]{2,1,0:T(8,128)(2,1)S(1)}, u32[]{:S(2)}, u32[]{:S(2)}) collective-permute-start(bf16[2,32,512]{2,1,0:T(8,128)(2,1)S(1)} %fusion.16), channel_id=1, source_target_pairs={{0,4},{4,0},{8,12},{12,8},{16,20},{20,16},{24,28},{28,24},{1,5},{5... | collective-permute-start | bytes 196616 | tf_op jit(solution)/shard_map/ppermute | solution.py:36
  27.9 4.6 %collective-permute-start.8 = (bf16[2,32,512]{2,1,0:T(8,128)(2,1)S(1)}, bf16[2,32,512]{2,1,0:T(8,128)(2,1)S(1)}, u32[]{:S(2)}, u32[]{:S(2)}) collective-permute-start(bf16[2,32,512]{2,1,0:T(8,128)(2,1)S(1)} %add_convert_fusion), channel_id=1, source_target_pairs={{0,24},{4,28},{8,0},{12,4},{16,8},{20,12},{24,16},{28,20},{1,25},{... | collective-permute-start | bytes 196616 | tf_op jit(solution)/shard_map/ppermute | solution.py:29
  29.8 6.2 %collective-permute-start.7 = (bf16[2,32,512]{2,1,0:T(8,128)(2,1)S(1)}, bf16[2,32,512]{2,1,0:T(8,128)(2,1)S(1)}, u32[]{:S(2)}, u32[]{:S(2)}) collective-permute-start(bf16[2,32,512]{2,1,0:T(8,128)(2,1)S(1)} %add_convert_fusion), channel_id=1, source_target_pairs={{0,16},{4,20},{8,24},{12,28},{16,0},{20,4},{24,8},{28,12},{1,17},{... | collective-permute-start | bytes 196616 | tf_op jit(solution)/shard_map/ppermute | solution.py:29
  29.8 6.2 %collective-permute-start.6 = (bf16[2,32,512]{2,1,0:T(8,128)(2,1)S(1)}, bf16[2,32,512]{2,1,0:T(8,128)(2,1)S(1)}, u32[]{:S(2)}, u32[]{:S(2)}) collective-permute-start(bf16[2,32,512]{2,1,0:T(8,128)(2,1)S(1)} %add_convert_fusion), channel_id=1, source_target_pairs={{0,8},{4,12},{8,16},{12,20},{16,24},{20,28},{24,0},{28,4},{1,9},{5... | collective-permute-start | bytes 196616 | tf_op jit(solution)/shard_map/ppermute | solution.py:29

commit v2 on v1

--- a/solution.py
+++ b/solution.py
@@ -6,14 +6,18 @@
 from jax.sharding import PartitionSpec as P
 
 
+def power_of_two(size):
+    return size & (size - 1) == 0
+
+
 def from_root(x, axis, size, root):
     me = lax.axis_index(axis)
-    bit = 1
-    if size & (size - 1) == 0:
-        while bit < size:
+    if power_of_two(size):
+        bit = size // 2
+        while bit:
             other = lax.ppermute(x, axis, [(i, i ^ bit) for i in range(size)])
             x = jnp.where((root & bit) == (me & bit), x, other)
-            bit *= 2
+            bit //= 2
         return x
     mine = x
     for k in range(1, size):
@@ -22,49 +26,53 @@
     return x
 
 
-def shift_outer(x, axis, outer, inner, k):
+def to(place, k, size):
+    return place ^ k if power_of_two(size) else (place + k) % size
+
+
+def slot(place, owner, size):
+    return place ^ owner if power_of_two(size) else (place - owner) % size
+
+
+def send_low(x, axis, outer, inner, k):
     pairs = [
-        (o * inner + n, (o + k) % outer * inner + n) for o in range(outer) for n in range(inner)
+        (o * inner + n, o * inner + to(n, k, inner)) for o in range(outer) for n in range(inner)
     ]
     return lax.ppermute(x, axis, pairs)
 
 
-def shift_inner(x, axis, outer, inner, k):
+def send_high(x, axis, outer, inner, k):
     pairs = [
-        (o * inner + n, o * inner + (n + k) % inner) for o in range(outer) for n in range(inner)
+        (o * inner + n, to(o, k, outer) * inner + n) for o in range(outer) for n in range(inner)
     ]
     return lax.ppermute(x, axis, pairs)
 
 
 def sum_over(parts, axis, outer, inner):
-    place = lax.axis_index(axis) // inner
+    index = lax.axis_index(axis)
+    place, row = index % inner, index // inner
     sent = parts.astype(jnp.bfloat16)
     total = lax.dynamic_index_in_dim(parts, place, 0, keepdims=False)
-    order = sorted(range(1, outer), key=lambda k: -min(k, outer - k))
-    for k in order:
-        chunk = lax.dynamic_index_in_dim(sent, (place + k) % outer, 0, keepdims=False)
-        total = total + shift_outer(chunk, axis, outer, inner, k).astype(jnp.float32)
+    for k in range(1, inner):
+        chunk = lax.dynamic_index_in_dim(sent, to(place, k, inner), 0, keepdims=False)
+        total = total + send_low(chunk, axis, outer, inner, k).astype(jnp.float32)
     mine = total.astype(jnp.bfloat16)
-    position = lax.axis_index(axis) % inner
-    pieces = [mine] + [shift_inner(mine, axis, outer, inner, k) for k in range(1, inner)]
-    if inner == 2:
+    pieces = [mine] + [send_high(mine, axis, outer, inner, k) for k in range(1, outer)]
+    if outer == 2:
         mine = (pieces[0].astype(jnp.float32) + pieces[1].astype(jnp.float32)).astype(jnp.bfloat16)
     else:
         ordered = jnp.stack(pieces)
         mine = sum(
-            lax.dynamic_index_in_dim(ordered, (position - n) % inner, 0, keepdims=False).astype(
+            lax.dynamic_index_in_dim(ordered, slot(row, o, outer), 0, keepdims=False).astype(
                 jnp.float32
             )
-            for n in range(inner)
+            for o in range(outer)
         ).astype(jnp.bfloat16)
-    gathered = {0: mine}
-    for k in order:
-        gathered[k] = shift_outer(mine, axis, outer, inner, k)
-    ordered = jnp.stack([gathered[k] for k in range(outer)])
+    ordered = jnp.stack([mine] + [send_low(mine, axis, outer, inner, k) for k in range(1, inner)])
     return jnp.stack(
         [
-            lax.dynamic_index_in_dim(ordered, (place - q) % outer, 0, keepdims=False)
-            for q in range(outer)
+            lax.dynamic_index_in_dim(ordered, slot(place, q, inner), 0, keepdims=False)
+            for q in range(inner)
         ]
     )
 
@@ -88,9 +96,9 @@
     left = left.reshape(2 * orbitals, points * 2 * orbitals)
     window = history.reshape(points * 2 * orbitals, second_time * orbitals)
     terms = jnp.dot(left, window, preferred_element_type=jnp.float32)
-    inner = max(d for d in range(1, math.isqrt(tint_size) + 1) if tint_size % d == 0)
-    outer = tint_size // inner
-    parts = terms.reshape(2, outer, orbitals // outer, second_time * orbitals).swapaxes(0, 1)
+    outer = max(d for d in range(1, math.isqrt(tint_size) + 1) if tint_size % d == 0)
+    inner = tint_size // outer
+    parts = terms.reshape(2, inner, orbitals // inner, second_time * orbitals).swapaxes(0, 1)
     summed = sum_over(parts, "tint", outer, inner)
     summed = summed.swapaxes(0, 1).reshape(2, orbitals, second_time * orbitals).astype(jnp.float32)
     flat = first_row.reshape(2, orbitals, second_time * orbitals)

time: 38.3 us -> 36.1 us (0.943)
  waiting for transfers between devices: 18.2 us -> 14.9 us
  other arithmetic: 2.17 us -> 3.2 us
  starting transfers between devices: 12.2 us -> 12.9 us
  local copies, waits for them, and re-layouts: 3.43 us -> 2.89 us
    ppermute x7, waiting for transfers between devices: 14.4 us -> 11 us  [the longest x6 7.86 us: send_low(): return lax.ppermute(x, axis, pairs)]
    reshape x1, local copies, waits for them, and re-layouts: 1.3 us -> 0.2 us  [shards(): window = history.reshape(points * 2 * orbitals, second_time * orbitals)]
    select_n x1, other arithmetic: 0.18 us -> 1.22 us  [from_root(): x = jnp.where(root & bit == me & bit, x, other)]
    ppermute x7, starting transfers between devices: 8.97 us -> 9.76 us  [the longest x6 7.11 us: send_low(): return lax.ppermute(x, axis, pairs)]
    unnamed x8 -> x10, local copies, waits for them, and re-layouts: 0.02 us -> 0.58 us
  transfers between devices with their start and end apart: 9 -> 9, of which waited for: 7 -> 9; matrix products, arithmetic and copies ran while one was open for 4% -> 1% of each run, Pallas kernels for 0% -> 0%
where the time goes in v2:
time: 36.1 us; the launch traced here: 35.9 us
  waiting for transfers between devices  14.9 us (41%)
  starting transfers between devices  12.9 us (36%)
  other arithmetic  3.2 us (9%)
  local copies, waits for them, and re-layouts  2.89 us (8%)
  matrix products  1.07 us (3%)
  between operations  0.96 us (3%)
    ppermute x6, waiting for transfers between devices, send_low(): return lax.ppermute(x, axis, pairs)  7.86 us
    ppermute x6, starting transfers between devices, send_low(): return lax.ppermute(x, axis, pairs)  7.11 us
    ppermute x2, waiting for transfers between devices, from_root(): other = lax.ppermute(x, axis, [(i, i ^ bit) for i in range(size)])  3.83 us
    ppermute x1, waiting for transfers between devices, send_high(): return lax.ppermute(x, axis, pairs)  3.19 us
    ppermute x2, starting transfers between devices, from_root(): other = lax.ppermute(x, axis, [(i, i ^ bit) for i in range(size)])  3.13 us
    ppermute x1, starting transfers between devices, send_high(): return lax.ppermute(x, axis, pairs)  2.65 us
    select_n x1, other arithmetic, from_root(): x = jnp.where(root & bit == me & bit, x, other)  1.22 us
    convert_element_type x1, local copies, waits for them, and re-layouts, shards(): lax.dynamic_slice_in_dim(first_row, offset, points, 2).astype(jnp.bfloat16)  1.17 us
  transfers between devices with their start and end apart: 9, of which 9 were waited for; matrix products, arithmetic and copies ran while one was open for 1% of the time, Pallas kernels for 0%

profile of v2, /device:TPU:0, one launch (start us, length us, event | category | flops | bytes accessed | tf_op | source)
XLA Modules:
  0.0 35.9 jit_solution(8719039633819588815)
XLA Ops:
  0.7 1.2 %dynamic-slice_convert_fusion = bf16[2,128,2,128]{3,2,1,0:T(2,128)(2,1)S(1)} fusion(f32[2,128,4,128]{3,2,1,0:T(4,128)} %param.7, s32[]{:T(128)S(6)} %select_n.54), kind=kLoop, calls=%fused_computation.16 | loop fusion | bytes 262148 | tf_op jit(solution)/shard_map/convert_element_type | solution.py:87
  1.9 3.1 %collective-permute-start = (bf16[2,128,2,128]{3,2,1,0:T(2,128)(2,1)S(1)}, bf16[2,128,2,128]{3,2,1,0:T(2,128)(2,1)S(1)}, u32[]{:S(2)}, u32[]{:S(2)}) collective-permute-start(bf16[2,128,2,128]{3,2,1,0:T(2,128)(2,1)S(1)} %dynamic-slice_convert_fusion), channel_id=1, source_target_pairs={{0,2},{1,3},{2,0},{3,1},{4,6},{5,7},{6,4},{7,5},{8,10},{9,11},{10,... | collective-permute-start | bytes 393224 | tf_op jit(solution)/shard_map/ppermute | solution.py:18
  5.0 3.5 %collective-permute-done = bf16[2,128,2,128]{3,2,1,0:T(2,128)(2,1)S(1)} collective-permute-done((bf16[2,128,2,128]{3,2,1,0:T(2,128)(2,1)S(1)}, bf16[2,128,2,128]{3,2,1,0:T(2,128)(2,1)S(1)}, u32[]{:S(2)}, u32[]{:S(2)}) %collective-permute-start) | collective-permute-done | bytes 131104 | tf_op jit(solution)/shard_map/ppermute | solution.py:18
  8.5 1.2 %broadcast_select_fusion = bf16[2,128,2,128]{3,2,1,0:T(2,128)(2,1)S(1)} fusion(bf16[2,128,2,128]{3,2,1,0:T(2,128)(2,1)S(1)} %collective-permute-done, pred[]{:T(512)S(6)} %eq.10, f32[2,128,4,128]{3,2,1,0:T(4,128)} %param.7, s32[]{:T(128)S(6)} %select_n.54), kind=kLoop, calls=%fused_computation.17 | loop fusion | flops 65536 | bytes 393221 | tf_op jit(solution)/shard_map/jit(_where)/select_n | solution.py:19
  10.0 0.6 %copy-done.3 = f32[128,128]{1,0:T(8,128)S(1)} copy-done((f32[128,128]{1,0:T(8,128)S(1)}, f32[128,128]{1,0:T(8,128)}, u32[]{:S(2)}) %copy-start.3) | copy-done | bytes 65560
  10.8 0.3 collective-permute-done.1
  11.7 0.3 pad_maximum_fusion.2
  12.5 0.3 fusion.21
  12.9 1.8 %collective-permute-start.2 = (bf16[2,32,512]{2,1,0:T(8,128)(2,1)S(1)}, bf16[2,32,512]{2,1,0:T(8,128)(2,1)S(1)}, u32[]{:S(2)}, u32[]{:S(2)}) collective-permute-start(bf16[2,32,512]{2,1,0:T(8,128)(2,1)S(1)} %get-tuple-element.15), channel_id=1, source_target_pairs={{0,4},{4,0},{8,12},{12,8},{16,20},{20,16},{24,28},{28,24},{1,5},{5... | collective-permute-start | bytes 196616 | tf_op jit(solution)/shard_map/ppermute | solution.py:41
  14.7 1.6 %collective-permute-start.3 = (bf16[2,32,512]{2,1,0:T(8,128)(2,1)S(1)}, bf16[2,32,512]{2,1,0:T(8,128)(2,1)S(1)}, u32[]{:S(2)}, u32[]{:S(2)}) collective-permute-start(bf16[2,32,512]{2,1,0:T(8,128)(2,1)S(1)} %get-tuple-element.17), channel_id=1, source_target_pairs={{0,8},{4,12},{8,0},{12,4},{16,24},{20,28},{24,16},{28,20},{1,9},{5... | collective-permute-start | bytes 196616 | tf_op jit(solution)/shard_map/ppermute | solution.py:41
  16.4 0.8 %collective-permute-done.2 = bf16[2,32,512]{2,1,0:T(8,128)(2,1)S(1)} collective-permute-done((bf16[2,32,512]{2,1,0:T(8,128)(2,1)S(1)}, bf16[2,32,512]{2,1,0:T(8,128)(2,1)S(1)}, u32[]{:S(2)}, u32[]{:S(2)}) %collective-permute-start.2) | collective-permute-done | bytes 65568 | tf_op jit(solution)/shard_map/ppermute | solution.py:41
  17.2 2.2 %collective-permute-done.3 = bf16[2,32,512]{2,1,0:T(8,128)(2,1)S(1)} collective-permute-done((bf16[2,32,512]{2,1,0:T(8,128)(2,1)S(1)}, bf16[2,32,512]{2,1,0:T(8,128)(2,1)S(1)}, u32[]{:S(2)}, u32[]{:S(2)}) %collective-permute-start.3) | collective-permute-done | bytes 65568 | tf_op jit(solution)/shard_map/ppermute | solution.py:41
  19.5 1.9 %collective-permute-done.4 = bf16[2,32,512]{2,1,0:T(8,128)(2,1)S(1)} collective-permute-done((bf16[2,32,512]{2,1,0:T(8,128)(2,1)S(1)}, bf16[2,32,512]{2,1,0:T(8,128)(2,1)S(1)}, u32[]{:S(2)}, u32[]{:S(2)}) %collective-permute-start.4) | collective-permute-done | bytes 65568 | tf_op jit(solution)/shard_map/ppermute | solution.py:41
  21.4 2.7 %collective-permute-start.5 = (bf16[2,32,512]{2,1,0:T(8,128)(2,1)S(1)}, bf16[2,32,512]{2,1,0:T(8,128)(2,1)S(1)}, u32[]{:S(2)}, u32[]{:S(2)}) collective-permute-start(bf16[2,32,512]{2,1,0:T(8,128)(2,1)S(1)} %fusion.16), channel_id=1, source_target_pairs={{0,16},{4,20},{8,24},{12,28},{16,0},{20,4},{24,8},{28,12},{1,17},{... | collective-permute-start | bytes 196616 | tf_op jit(solution)/shard_map/ppermute | solution.py:48
  24.1 3.2 %collective-permute-done.5 = bf16[2,32,512]{2,1,0:T(8,128)(2,1)S(1)} collective-permute-done((bf16[2,32,512]{2,1,0:T(8,128)(2,1)S(1)}, bf16[2,32,512]{2,1,0:T(8,128)(2,1)S(1)}, u32[]{:S(2)}, u32[]{:S(2)}) %collective-permute-start.5) | collective-permute-done | bytes 65568 | tf_op jit(solution)/shard_map/ppermute | solution.py:48
  27.3 0.7 %collective-permute-start.6 = (bf16[2,32,512]{2,1,0:T(8,128)(2,1)S(1)}, bf16[2,32,512]{2,1,0:T(8,128)(2,1)S(1)}, u32[]{:S(2)}, u32[]{:S(2)}) collective-permute-start(bf16[2,32,512]{2,1,0:T(8,128)(2,1)S(1)} %add_convert_fusion), channel_id=1, source_target_pairs={{0,4},{4,0},{8,12},{12,8},{16,20},{20,16},{24,28},{28,24},{1,5},{5... | collective-permute-start | bytes 196616 | tf_op jit(solution)/shard_map/ppermute | solution.py:41
  28.0 0.4 %collective-permute-start.7 = (bf16[2,32,512]{2,1,0:T(8,128)(2,1)S(1)}, bf16[2,32,512]{2,1,0:T(8,128)(2,1)S(1)}, u32[]{:S(2)}, u32[]{:S(2)}) collective-permute-start(bf16[2,32,512]{2,1,0:T(8,128)(2,1)S(1)} %add_convert_fusion), channel_id=1, source_target_pairs={{0,8},{4,12},{8,0},{12,4},{16,24},{20,28},{24,16},{28,20},{1,9},{5... | collective-permute-start | bytes 196616 | tf_op jit(solution)/shard_map/ppermute | solution.py:41
  28.4 2.4 %collective-permute-start.8 = (bf16[2,32,512]{2,1,0:T(8,128)(2,1)S(1)}, bf16[2,32,512]{2,1,0:T(8,128)(2,1)S(1)}, u32[]{:S(2)}, u32[]{:S(2)}) collective-permute-start(bf16[2,32,512]{2,1,0:T(8,128)(2,1)S(1)} %add_convert_fusion), channel_id=1, source_target_pairs={{0,12},{4,8},{8,4},{12,0},{16,28},{20,24},{24,20},{28,16},{1,13},{... | collective-permute-start | bytes 196616 | tf_op jit(solution)/shard_map/ppermute | solution.py:41
  30.9 0.7 %collective-permute-done.6 = bf16[2,32,512]{2,1,0:T(8,128)(2,1)S(1)} collective-permute-done((bf16[2,32,512]{2,1,0:T(8,128)(2,1)S(1)}, bf16[2,32,512]{2,1,0:T(8,128)(2,1)S(1)}, u32[]{:S(2)}, u32[]{:S(2)}) %collective-permute-start.6) | collective-permute-done | bytes 65568 | tf_op jit(solution)/shard_map/ppermute | solution.py:41
  31.6 0.6 %collective-permute-done.7 = bf16[2,32,512]{2,1,0:T(8,128)(2,1)S(1)} collective-permute-done((bf16[2,32,512]{2,1,0:T(8,128)(2,1)S(1)}, bf16[2,32,512]{2,1,0:T(8,128)(2,1)S(1)}, u32[]{:S(2)}, u32[]{:S(2)}) %collective-permute-start.7) | collective-permute-done | bytes 65568 | tf_op jit(solution)/shard_map/ppermute | solution.py:41
  32.3 1.5 %collective-permute-done.8 = bf16[2,32,512]{2,1,0:T(8,128)(2,1)S(1)} collective-permute-done((bf16[2,32,512]{2,1,0:T(8,128)(2,1)S(1)}, bf16[2,32,512]{2,1,0:T(8,128)(2,1)S(1)}, u32[]{:S(2)}, u32[]{:S(2)}) %collective-permute-start.8) | collective-permute-done | bytes 65568 | tf_op jit(solution)/shard_map/ppermute | solution.py:41
  34.0 0.4 %fusion.3 = f32[128,512]{1,0:T(8,128)S(1)} fusion(f32[128,512]{1,0:T(8,128)S(1)} %bitcast.67, f32[128,128]{1,0:T(8,128)S(1)} %copy-done, f32[16,8,4,128]{3,2,1,0:T(4,128)S(1)} %bitcast.64, f32[16,8,4,128]{3,2,1,0:T(4,128)S(1)} %bitcast.62), kind=kOutput, calls=%fused_computation.5 | convolution fusion | flops 100859904 | bytes 1114112 | tf_op jit(solution)/shard_map/dot_general | solution.py:106
  34.5 0.4 %fusion.1 = f32[128,512]{1,0:T(8,128)S(1)} fusion(f32[128,512]{1,0:T(8,128)S(1)} %bitcast.66, f32[128,128]{1,0:T(8,128)S(1)} %copy-done, f32[16,8,4,128]{3,2,1,0:T(4,128)S(1)} %bitcast.65, f32[16,8,4,128]{3,2,1,0:T(4,128)S(1)} %bitcast.63), kind=kOutput, calls=%fused_computation.2 | convolution fusion | flops 100859904 | bytes 1114112 | tf_op jit(solution)/shard_map/dot_general | solution.py:105
  35.0 0.9 %pad_maximum_fusion = f32[2,128,4,128]{3,2,1,0:T(4,128)} fusion(f32[1,128,4,128]{3,2,1,0:T(4,128)S(1)} %stack.62, f32[1,128,4,128]{3,2,1,0:T(4,128)S(1)} %stack.61), kind=kLoop, calls=%fused_computation.6 | loop fusion | flops 131072 | bytes 1048576 | tf_op jit(solution)/shard_map/stack | solution.py:109
  (33 shorter events, 2.2 us)
Async XLA Ops:
  0.0 34.0 %copy-start = (f32[128,128]{1,0:T(8,128)S(1)}, f32[128,128]{1,0:T(8,128)}, u32[]{:S(2)}) copy-start(f32[128,128]{1,0:T(8,128)} %param.8) | copy-start | bytes 196612
  0.0 10.5 %copy-start.2 = (bf16[2,2,128,4,128]{4,3,2,1,0:T(4,128)(2,1)S(1)}, bf16[2,2,128,4,128]{4,3,2,1,0:T(4,128)(2,1)}, u32[]{:S(2)}) copy-start(bf16[2,2,128,4,128]{4,3,2,1,0:T(4,128)(2,1)} %param.6) | copy-start | bytes 1572868
  1.9 6.6 %collective-permute-start = (bf16[2,128,2,128]{3,2,1,0:T(2,128)(2,1)S(1)}, bf16[2,128,2,128]{3,2,1,0:T(2,128)(2,1)S(1)}, u32[]{:S(2)}, u32[]{:S(2)}) collective-permute-start(bf16[2,128,2,128]{3,2,1,0:T(2,128)(2,1)S(1)} %dynamic-slice_convert_fusion), channel_id=1, source_target_pairs={{0,2},{1,3},{2,0},{3,1},{4,6},{5,7},{6,4},{7,5},{8,10},{9,11},{10,... | collective-permute-start | bytes 393224 | tf_op jit(solution)/shard_map/ppermute | solution.py:18
  5.0 4.8 %copy-start.4 = (s32[128]{0:T(128)S(1)}, s32[128]{0:T(128)}, u32[]{:S(2)}) copy-start(s32[128]{0:T(128)} %param.10) | copy-start | bytes 1540
  9.7 0.8 %copy-start.3 = (f32[128,128]{1,0:T(8,128)S(1)}, f32[128,128]{1,0:T(8,128)}, u32[]{:S(2)}) copy-start(f32[128,128]{1,0:T(8,128)} %param.9) | copy-start | bytes 196612
  9.7 1.4 %collective-permute-start.1 = (bf16[2,128,2,128]{3,2,1,0:T(2,128)(2,1)S(1)}, bf16[2,128,2,128]{3,2,1,0:T(2,128)(2,1)S(1)}, u32[]{:S(2)}, u32[]{:S(2)}) collective-permute-start(bf16[2,128,2,128]{3,2,1,0:T(2,128)(2,1)S(1)} %broadcast_select_fusion), channel_id=1, source_target_pairs={{0,1},{1,0},{2,3},{3,2},{4,5},{5,4},{6,7},{7,6},{8,9},{9,8},{10,11... | collective-permute-start | bytes 393224 | tf_op jit(solution)/shard_map/ppermute | solution.py:18
  12.9 18.0 %copy-start.1 = (f32[2,128,4,128]{3,2,1,0:T(4,128)S(1)}, f32[2,128,4,128]{3,2,1,0:T(4,128)}, u32[]{:S(2)}) copy-start(f32[2,128,4,128]{3,2,1,0:T(4,128)} %param.7) | copy-start | bytes 1572868
  12.9 4.3 %collective-permute-start.2 = (bf16[2,32,512]{2,1,0:T(8,128)(2,1)S(1)}, bf16[2,32,512]{2,1,0:T(8,128)(2,1)S(1)}, u32[]{:S(2)}, u32[]{:S(2)}) collective-permute-start(bf16[2,32,512]{2,1,0:T(8,128)(2,1)S(1)} %get-tuple-element.15), channel_id=1, source_target_pairs={{0,4},{4,0},{8,12},{12,8},{16,20},{20,16},{24,28},{28,24},{1,5},{5... | collective-permute-start | bytes 196616 | tf_op jit(solution)/shard_map/ppermute | solution.py:41
  14.7 4.8 %collective-permute-start.3 = (bf16[2,32,512]{2,1,0:T(8,128)(2,1)S(1)}, bf16[2,32,512]{2,1,0:T(8,128)(2,1)S(1)}, u32[]{:S(2)}, u32[]{:S(2)}) collective-permute-start(bf16[2,32,512]{2,1,0:T(8,128)(2,1)S(1)} %get-tuple-element.17), channel_id=1, source_target_pairs={{0,8},{4,12},{8,0},{12,4},{16,24},{20,28},{24,16},{28,20},{1,9},{5... | collective-permute-start | bytes 196616 | tf_op jit(solution)/shard_map/ppermute | solution.py:41
  16.2 5.2 %collective-permute-start.4 = (bf16[2,32,512]{2,1,0:T(8,128)(2,1)S(1)}, bf16[2,32,512]{2,1,0:T(8,128)(2,1)S(1)}, u32[]{:S(2)}, u32[]{:S(2)}) collective-permute-start(bf16[2,32,512]{2,1,0:T(8,128)(2,1)S(1)} %get-tuple-element.16), channel_id=1, source_target_pairs={{0,12},{4,8},{8,4},{12,0},{16,28},{20,24},{24,20},{28,16},{1,13},{... | collective-permute-start | bytes 196616 | tf_op jit(solution)/shard_map/ppermute | solution.py:41
  21.4 5.8 %collective-permute-start.5 = (bf16[2,32,512]{2,1,0:T(8,128)(2,1)S(1)}, bf16[2,32,512]{2,1,0:T(8,128)(2,1)S(1)}, u32[]{:S(2)}, u32[]{:S(2)}) collective-permute-start(bf16[2,32,512]{2,1,0:T(8,128)(2,1)S(1)} %fusion.16), channel_id=1, source_target_pairs={{0,16},{4,20},{8,24},{12,28},{16,0},{20,4},{24,8},{28,12},{1,17},{... | collective-permute-start | bytes 196616 | tf_op jit(solution)/shard_map/ppermute | solution.py:48
  27.3 4.3 %collective-permute-start.6 = (bf16[2,32,512]{2,1,0:T(8,128)(2,1)S(1)}, bf16[2,32,512]{2,1,0:T(8,128)(2,1)S(1)}, u32[]{:S(2)}, u32[]{:S(2)}) collective-permute-start(bf16[2,32,512]{2,1,0:T(8,128)(2,1)S(1)} %add_convert_fusion), channel_id=1, source_target_pairs={{0,4},{4,0},{8,12},{12,8},{16,20},{20,16},{24,28},{28,24},{1,5},{5... | collective-permute-start | bytes 196616 | tf_op jit(solution)/shard_map/ppermute | solution.py:41
  28.0 4.3 %collective-permute-start.7 = (bf16[2,32,512]{2,1,0:T(8,128)(2,1)S(1)}, bf16[2,32,512]{2,1,0:T(8,128)(2,1)S(1)}, u32[]{:S(2)}, u32[]{:S(2)}) collective-permute-start(bf16[2,32,512]{2,1,0:T(8,128)(2,1)S(1)} %add_convert_fusion), channel_id=1, source_target_pairs={{0,8},{4,12},{8,0},{12,4},{16,24},{20,28},{24,16},{28,20},{1,9},{5... | collective-permute-start | bytes 196616 | tf_op jit(solution)/shard_map/ppermute | solution.py:41
  28.4 5.4 %collective-permute-start.8 = (bf16[2,32,512]{2,1,0:T(8,128)(2,1)S(1)}, bf16[2,32,512]{2,1,0:T(8,128)(2,1)S(1)}, u32[]{:S(2)}, u32[]{:S(2)}) collective-permute-start(bf16[2,32,512]{2,1,0:T(8,128)(2,1)S(1)} %add_convert_fusion), channel_id=1, source_target_pairs={{0,12},{4,8},{8,4},{12,0},{16,28},{20,24},{24,20},{28,16},{1,13},{... | collective-permute-start | bytes 196616 | tf_op jit(solution)/shard_map/ppermute | solution.py:41

commit v3 on v2

v3 whole, which is shorter than its diff:
```python
import functools
import math

import jax
import jax.numpy as jnp
from jax import lax
from jax.experimental import pallas as pl
from jax.experimental.pallas import tpu as pltpu
from jax.sharding import PartitionSpec as P

VMEM = pl.BlockSpec(memory_space=pltpu.VMEM)
SMEM = pl.BlockSpec(memory_space=pltpu.SMEM)
ANY = pl.BlockSpec(memory_space=pl.ANY)


def power_of_two(size):
    return size & (size - 1) == 0


def to(place, k, size):
    return place ^ k if power_of_two(size) else lax.rem(place + k, size)


def slot(place, owner, size):
    return place ^ owner if power_of_two(size) else (place - owner) % size


def send_low(x, axis, outer, inner, k):
    n = range(inner)
    target = [i ^ k if power_of_two(inner) else (i + k) % inner for i in n]
    pairs = [(o * inner + i, o * inner + target[i]) for o in range(outer) for i in n]
    return lax.ppermute(x, axis, pairs)


def send_high(x, axis, outer, inner, k):
    target = [o ^ k if power_of_two(outer) else (o + k) % outer for o in range(outer)]
    pairs = [(o * inner + i, target[o] * inner + i) for o in range(outer) for i in range(inner)]
    return lax.ppermute(x, axis, pairs)


def shape_of(rows, columns, kind):
    return jax.ShapeDtypeStruct((rows, columns), kind)


def room(mebibytes):
    return pltpu.CompilerParams(vmem_limit_bytes=mebibytes << 20)


def cost(flops, moved):
    return pl.CostEstimate(flops=flops, bytes_accessed=moved, transcendentals=0)


def piece_kernel(points, orbitals, second_time, block_ref, row_ref, piece_ref):
    groups = second_time // points
    block = block_ref[...]
    group = block & (groups - 1) if power_of_two(groups) else lax.rem(block, groups)
    for p in range(points):
        for part in range(2):
            start = part * orbitals * second_time + p
            rows = row_ref[pl.ds(start, orbitals, stride=second_time), :]
            for g in range(1, groups):
                here = pl.ds(start + g * points, orbitals, stride=second_time)
                rows = jnp.where(group == g, row_ref[here, :], rows)
            at = (p * 2 + part) * orbitals
            piece_ref[at : at + orbitals, :] = rows.astype(jnp.bfloat16)


def pick_kernel(points, second_time, bit, axis, block_ref, mine_ref, other_ref, out_ref):
    root = lax.div(block_ref[0] * points, second_time)
    mine = (root & bit) == (lax.axis_index(axis) & bit)

    @pl.when(mine)
    def _():
        out_ref[...] = mine_ref[...]

    @pl.when(jnp.logical_not(mine))
    def _():
        out_ref[...] = other_ref[...]


def ready_kernel(
    points, orbitals, second_time, inner, axis,
    block_ref, start_ref, coupling_ref, hamiltonian_ref, history_ref, row_ref,
    window_ref, scaled_ref, base_ref,
):
    n, width = orbitals, orbitals // inner
    place = lax.rem(lax.axis_index(axis), inner)
    first = block_ref[0] * points
    for k in range(inner):
        at = pl.multiple_of(to(place, k, inner) * width, width)
        rows = -coupling_ref[pl.ds(at, width), :]
        begins = start_ref[pl.ds(at, width), :]
        for p in range(points):
            live = (first + p >= begins).astype(jnp.float32)
            scaled_ref[(k * points + p) * width : (k * points + p + 1) * width, :] = rows * live
    for part in range(2):
        other = 1 - part
        now, turned = (
            jnp.concatenate(
                [
                    row_ref[pl.ds(which * n * second_time + t, n, stride=second_time), :]
                    for t in range(second_time)
                ],
                1,
            )
            for which in (part, other)
        )
        hg = jnp.dot(
            hamiltonian_ref[...],
            turned,
            precision=lax.Precision.HIGHEST,
            preferred_element_type=jnp.float32,
        )
        base_ref[part * n : (part + 1) * n, :] = now + 0.25 * hg if part == 0 else now - 0.25 * hg
    rows = points * 2 * n
    spread = history_ref[...].astype(jnp.float32).reshape(rows, second_time, n)
    for t in range(second_time):
        window_ref[:, t * n : (t + 1) * n] = spread[:, t, :].astype(jnp.bfloat16)


def terms_kernel(
    points, orbitals, second_time, bit, inner, tint, tsec,
    block_ref, mine_ref, other_ref, scaled_ref, window_ref, own_ref, *rest,
):
    *sent_refs, left = rest
    n, width = orbitals, orbitals // inner
    root = lax.div(block_ref[0] * points, second_time)
    mine = (root & bit) == (lax.axis_index(tsec) & bit)
    place = lax.rem(lax.axis_index(tint), inner)
    for k in range(inner):
        at = pl.multiple_of(to(place, k, inner) * width, width)
        low = k * 2 * width
        for p in range(points):
            real, imag = (
                jnp.where(
                    mine,
                    mine_ref[pl.ds((p * 2 + part) * n + at, width), :].astype(jnp.float32),
                    other_ref[pl.ds((p * 2 + part) * n + at, width), :].astype(jnp.float32),
                )
                for part in range(2)
            )
            scaled = scaled_ref[(k * points + p) * width : (k * points + p + 1) * width, :]
            factor = scaled * (real * real + imag * imag)
            sr, si = factor * real, factor * imag
            c = p * 2 * n
            left[low : low + width, c : c + n] = sr.astype(jnp.bfloat16)
            left[low : low + width, c + n : c + 2 * n] = (-si).astype(jnp.bfloat16)
            left[low + width : low + 2 * width, c : c + n] = si.astype(jnp.bfloat16)
            left[low + width : low + 2 * width, c + n : c + 2 * n] = sr.astype(jnp.bfloat16)
    product = jnp.dot(left[...], window_ref[...], preferred_element_type=jnp.float32)
    own_ref[...] = product[: 2 * width, :]
    for k in range(1, inner):
        sent_refs[k - 1][...] = product[k * 2 * width : (k + 1) * 2 * width, :].astype(jnp.bfloat16)


def update_kernel(orbitals, second_time, inner, axis, base_ref, *rest):
    *chunk_refs, out_ref, held, sem = rest
    n, width = orbitals, orbitals // inner
    place = lax.rem(lax.axis_index(axis), inner)
    copies = []
    for k in range(inner):
        owner = to(place, k, inner) if power_of_two(inner) else lax.rem(place - k + inner, inner)
        at = pl.multiple_of(owner * width, width)
        terms = chunk_refs[k][...].astype(jnp.float32)
        for part in range(2):
            base = base_ref[pl.ds(pl.multiple_of(part * n + at, width), width), :]
            if part == 0:
                new = base + 0.25 * terms[width:, :]
            else:
                new = base - 0.25 * terms[:width, :]
            start = pl.multiple_of((part * n + at) * second_time, width * second_time)
            for t in range(second_time):
                held[pl.ds(start + t, width, stride=second_time), :] = new[:, t * n : (t + 1) * n]
            rows = pl.ds(start, width * second_time)
            copy = pltpu.make_async_copy(held.at[rows], out_ref.at[rows], sem.at[2 * k + part])
            copy.start()
            copies.append(copy)
    for copy in copies:
        copy.wait()


def shards(tint_size, tsec_size, history, first_row, hamiltonian, coupling, window_start, block_time):
    points, _, n, second_time, _ = history.shape
    outer = max(d for d in range(1, math.isqrt(tint_size) + 1) if tint_size % d == 0)
    inner = tint_size // outer
    width = n // inner
    sizes = (points, n, second_time)
    rows = 2 * n * second_time
    flat = first_row.reshape(rows, n)
    piece = pl.pallas_call(
        functools.partial(piece_kernel, *sizes),
        out_shape=shape_of(points * 2 * n, n, jnp.bfloat16),
        in_specs=[VMEM, VMEM],
        out_specs=VMEM,
        compiler_params=room(8),
        cost_estimate=cost(0, 4 * rows * n),
    )(block_time.reshape(1, 1), flat)
    window, scaled, base = pl.pallas_call(
        functools.partial(ready_kernel, *sizes, inner, "tint"),
        out_shape=(
            shape_of(points * 2 * n, second_time * n, jnp.bfloat16),
            shape_of(points * n, n, jnp.float32),
            shape_of(2 * n, second_time * n, jnp.float32),
        ),
        in_specs=[SMEM] + [VMEM] * 5,
        out_specs=(VMEM, VMEM, VMEM),
        compiler_params=room(8),
        cost_estimate=cost(24 * n * n * n * second_time, 8 * rows * n),
    )(
        block_time,
        window_start.reshape(n, 1),
        coupling,
        hamiltonian,
        history.reshape(points * rows, n),
        flat,
    )
    bit = tsec_size // 2
    other, made = piece, None
    while bit:
        other = lax.ppermute(piece, "tsec", [(i, i ^ bit) for i in range(tsec_size)])
        if not made:
            other, *made = lax.optimization_barrier((other, window, scaled, base))
            window, scaled, base = made
        if bit == 1:
            break
        piece = pl.pallas_call(
            functools.partial(pick_kernel, points, second_time, bit, "tsec"),
            out_shape=shape_of(points * 2 * n, n, jnp.bfloat16),
            in_specs=[SMEM, VMEM, VMEM],
            out_specs=VMEM,
            compiler_params=room(8),
            cost_estimate=cost(0, 4 * points * n * n),
        )(block_time, piece, other)
        bit //= 2
    own, *sent = pl.pallas_call(
        functools.partial(terms_kernel, *sizes, bit, inner, "tint", "tsec"),
        out_shape=[shape_of(2 * width, second_time * n, jnp.float32)]
        + [shape_of(2 * width, second_time * n, jnp.bfloat16)] * (inner - 1),
        in_specs=[SMEM] + [VMEM] * 4,
        out_specs=[VMEM] * inner,
        scratch_shapes=[pltpu.VMEM((2 * n, points * 2 * n), jnp.bfloat16)],
        compiler_params=room(8),
        cost_estimate=cost(8 * points * n * n * n * second_time, 4 * rows * n),
    )(block_time, piece, other, scaled, window)
    total = own
    for k in range(1, inner):
        total = total + send_low(sent[k - 1], "tint", outer, inner, k).astype(jnp.float32)
    mine = total.astype(jnp.bfloat16)
    pieces = [mine] + [send_high(mine, "tint", outer, inner, k) for k in range(1, outer)]
    if outer == 2:
        mine = (pieces[0].astype(jnp.float32) + pieces[1].astype(jnp.float32)).astype(jnp.bfloat16)
    else:
        ordered = jnp.stack(pieces)
        high = lax.axis_index("tint") // inner
        mine = sum(
            lax.dynamic_index_in_dim(ordered, slot(high, o, outer), 0, keepdims=False).astype(
                jnp.float32
            )
            for o in range(outer)
        ).astype(jnp.bfloat16)
    chunks = [mine] + [send_low(mine, "tint", outer, inner, k) for k in range(1, inner)]
    new = pl.pallas_call(
        functools.partial(update_kernel, n, second_time, inner, "tint"),
        out_shape=shape_of(rows, n, jnp.float32),
        in_specs=[VMEM] * (1 + inner),
        out_specs=ANY,
        scratch_shapes=[
            pltpu.VMEM((rows, n), jnp.float32),
            pltpu.SemaphoreType.DMA((2 * inner,)),
        ],
        compiler_params=room(8),
        cost_estimate=cost(4 * rows * n, 8 * rows * n),
    )(base, *chunks)
    return new.reshape(first_row.shape)


def solution(mesh):
    tint_size, tsec_size = mesh.shape["tint"], mesh.shape["tsec"]

    def step(*arrays):
        return shards(tint_size, tsec_size, *arrays)

    return jax.shard_map(
        step,
        mesh=mesh,
        in_specs=(
            P("tint", None, None, "tsec", None),
            P(None, None, "tsec", None),
            P(),
            P(),
            P(),
            P("tint"),
        ),
        out_specs=P(None, None, "tsec", None),
        check_vma=False,
    )
```

time: 36.1 us -> 32.1 us (0.89)
  other arithmetic: 3.2 us -> 0.05 us
  Pallas kernels: 0 us -> 2.78 us
  waiting for transfers between devices: 14.9 us -> 13.2 us
  matrix products: 1.07 us -> 0 us
  local copies, waits for them, and re-layouts: 2.89 us -> 2.2 us
    pallas_call x0 -> x5, Pallas kernels: none -> 2.78 us  [the longest x1 1.47 us: shards(): pl.pallas_call(functools.partial(ready_kernel, *sizes, inner, 'tint'), ou...]
    ppermute x2, waiting for transfers between devices: 3.83 us -> 2.17 us  [shards(): lax.ppermute(piece, 'tsec', [(i, i ^ bit) for i in range(tsec_size)])]
    unnamed x10 -> x12, local copies, waits for them, and re-layouts: 0.58 us -> 2.09 us
    convert_element_type x2 -> x0, local copies, waits for them, and re-layouts: 1.28 us -> none  [the longest x1 1.17 us: shards(): lax.dynamic_slice_in_dim(first_row, offset, points, 2).astype(jnp.bfloat16)]
    another operation x3 -> x0, other arithmetic: 1.23 us -> none  [the longest x1 0.92 us: shards(): return jnp.stack([advanced_real, advanced_imag]).reshape(first_row.shape)]
    select_n x1 -> x0, other arithmetic: 1.22 us -> none  [from_root(): x = jnp.where(root & bit == me & bit, x, other)]
    dot_general x3 -> x0, matrix products: 1.07 us -> none  [the longest x1 0.39 us: shards(): hg_imag = jnp.dot(hamiltonian, flat[1], precision=lax.Precision.HIGHEST)]
    another operation x6 -> x0, local copies, waits for them, and re-layouts: 0.71 us -> none  [the longest x4 0.53 us: shards(): left = jnp.stack([jnp.stack([sr, -si], 2), jnp.stack([si, sr], 2)])]
  transfers between devices with their start and end apart: 9 -> 9, of which waited for: 9 -> 8; matrix products, arithmetic and copies ran while one was open for 1% -> 0% of each run, Pallas kernels for 0% -> 5%
where the time goes in v3:
time: 32.1 us; the launch traced here: 31.8 us
  waiting for transfers between devices  13.2 us (41%)
  starting transfers between devices  12.9 us (40%)
  Pallas kernels  2.78 us (9%)
  local copies, waits for them, and re-layouts  2.2 us (7%)
  between operations  0.75 us (2%)
    ppermute x6, waiting for transfers between devices, send_low(): return lax.ppermute(x, axis, pairs)  7.83 us
    ppermute x6, starting transfers between devices, send_low(): return lax.ppermute(x, axis, pairs)  7.11 us
    ppermute x1, waiting for transfers between devices, send_high(): return lax.ppermute(x, axis, pairs)  3.18 us
    ppermute x2, starting transfers between devices, shards(): lax.ppermute(piece, 'tsec', [(i, i ^ bit) for i in range(tsec_size)])  3.13 us
    ppermute x1, starting transfers between devices, send_high(): return lax.ppermute(x, axis, pairs)  2.66 us
    ppermute x2, waiting for transfers between devices, shards(): lax.ppermute(piece, 'tsec', [(i, i ^ bit) for i in range(tsec_size)])  2.17 us
    unnamed x12, local copies, waits for them, and re-layouts  2.09 us
    pallas_call x1, Pallas kernels, shards(): pl.pallas_call(functools.partial(ready_kernel, *sizes, inner, 'tint'), ou...  1.47 us
  transfers between devices with their start and end apart: 9, of which 8 were waited for; matrix products, arithmetic and copies ran while one was open for 0% of the time, Pallas kernels for 5%

profile of v3, /device:TPU:0, one launch (start us, length us, event | category | flops | bytes accessed | tf_op | source)
XLA Modules:
  0.0 31.8 jit_solution(14784719126177933180)
XLA Ops:
  0.7 1.0 %copy-done = f32[2,128,4,128]{3,2,1,0:T(4,128)S(1)} copy-done((f32[2,128,4,128]{3,2,1,0:T(4,128)S(1)}, f32[2,128,4,128]{3,2,1,0:T(4,128)}, u32[]{:S(2)}) %copy-start) | copy-done | bytes 524312
  1.7 0.1 shard_map.64.mine_ref
  1.8 3.1 %collective-permute-start = (bf16[512,128]{1,0:T(8,128)(2,1)S(1)}, bf16[512,128]{1,0:T(8,128)(2,1)S(1)}, u32[]{:S(2)}, u32[]{:S(2)}) collective-permute-start(bf16[512,128]{1,0:T(8,128)(2,1)S(1)} %shard_map.64.mine_ref), channel_id=1, source_target_pairs={{0,2},{1,3},{2,0},{3,1},{4,6},{5,7},{6,4},{7,5},{8,10},{9,11},{10,... | collective-permute-start | bytes 393224 | tf_op jit(solution)/shard_map/ppermute | solution.py:220
  4.9 0.1 copy.7.start_ref
  5.0 1.0 %copy-done.2 = bf16[2,2,128,4,128]{4,3,2,1,0:T(4,128)(2,1)S(1)} copy-done((bf16[2,2,128,4,128]{4,3,2,1,0:T(4,128)(2,1)S(1)}, bf16[2,2,128,4,128]{4,3,2,1,0:T(4,128)(2,1)}, u32[]{:S(2)}) %copy-start.2) | copy-done | bytes 524312
  6.1 1.5 %shard_map.65 = (bf16[512,512]{1,0:T(8,128)(2,1)S(1)}, f32[256,128]{1,0:T(8,128)S(1)}, f32[256,512]{1,0:T(8,128)S(1)}) custom-call(s32[1]{0:T(128)} %copy.8.block_ref, s32[128,1]{1,0:T(8,128)S(1)} %copy.7.start_ref, f32[128,128]{1,0:T(8,128)S(1)} %copy-done.3, f32[128,128]{1,0:T(8,128)S(1)} %copy-done.4, bf16[2048,128]{1,0:T(8,128)(2,1)S(1)} %bitcast.8, ...), custom_call_target="tpu_custom_call" | custom-call | flops 201326592 | bytes 1048576 | tf_op jit(solution)/shard_map/pallas_call | solution.py:198
  7.5 0.8 %collective-permute-done.other_ref = bf16[512,128]{1,0:T(8,128)(2,1)S(1)} collective-permute-done((bf16[512,128]{1,0:T(8,128)(2,1)S(1)}, bf16[512,128]{1,0:T(8,128)(2,1)S(1)}, u32[]{:S(2)}, u32[]{:S(2)}) %collective-permute-start) | collective-permute-done | bytes 131104 | tf_op jit(solution)/shard_map/ppermute | solution.py:220
  8.4 0.1 collective-permute-start.1
  8.5 1.3 %collective-permute-done.1.other_ref = bf16[512,128]{1,0:T(8,128)(2,1)S(1)} collective-permute-done((bf16[512,128]{1,0:T(8,128)(2,1)S(1)}, bf16[512,128]{1,0:T(8,128)(2,1)S(1)}, u32[]{:S(2)}, u32[]{:S(2)}) %collective-permute-start.1) | collective-permute-done | bytes 131104 | tf_op jit(solution)/shard_map/ppermute | solution.py:220
  9.8 0.3 shard_map.67
  10.1 1.8 %collective-permute-start.2 = (bf16[64,512]{1,0:T(8,128)(2,1)S(1)}, bf16[64,512]{1,0:T(8,128)(2,1)S(1)}, u32[]{:S(2)}, u32[]{:S(2)}) collective-permute-start(bf16[64,512]{1,0:T(8,128)(2,1)S(1)} %get-tuple-element.24), channel_id=1, source_target_pairs={{0,4},{4,0},{8,12},{12,8},{16,20},{20,16},{24,28},{28,24},{1,5},{5... | collective-permute-start | bytes 196616 | tf_op jit(solution)/shard_map/ppermute | solution.py:32
  11.9 1.6 %collective-permute-start.3 = (bf16[64,512]{1,0:T(8,128)(2,1)S(1)}, bf16[64,512]{1,0:T(8,128)(2,1)S(1)}, u32[]{:S(2)}, u32[]{:S(2)}) collective-permute-start(bf16[64,512]{1,0:T(8,128)(2,1)S(1)} %get-tuple-element.25), channel_id=1, source_target_pairs={{0,8},{4,12},{8,0},{12,4},{16,24},{20,28},{24,16},{28,20},{1,9},{5... | collective-permute-start | bytes 196616 | tf_op jit(solution)/shard_map/ppermute | solution.py:32
  13.5 0.2 collective-permute-start.4
  13.7 0.8 %collective-permute-done.2 = bf16[64,512]{1,0:T(8,128)(2,1)S(1)} collective-permute-done((bf16[64,512]{1,0:T(8,128)(2,1)S(1)}, bf16[64,512]{1,0:T(8,128)(2,1)S(1)}, u32[]{:S(2)}, u32[]{:S(2)}) %collective-permute-start.2) | collective-permute-done | bytes 65568 | tf_op jit(solution)/shard_map/ppermute | solution.py:32
  14.5 2.2 %collective-permute-done.3 = bf16[64,512]{1,0:T(8,128)(2,1)S(1)} collective-permute-done((bf16[64,512]{1,0:T(8,128)(2,1)S(1)}, bf16[64,512]{1,0:T(8,128)(2,1)S(1)}, u32[]{:S(2)}, u32[]{:S(2)}) %collective-permute-start.3) | collective-permute-done | bytes 65568 | tf_op jit(solution)/shard_map/ppermute | solution.py:32
  16.7 1.9 %collective-permute-done.4 = bf16[64,512]{1,0:T(8,128)(2,1)S(1)} collective-permute-done((bf16[64,512]{1,0:T(8,128)(2,1)S(1)}, bf16[64,512]{1,0:T(8,128)(2,1)S(1)}, u32[]{:S(2)}, u32[]{:S(2)}) %collective-permute-start.4) | collective-permute-done | bytes 65568 | tf_op jit(solution)/shard_map/ppermute | solution.py:32
  18.7 2.7 %collective-permute-start.5 = (bf16[64,512]{1,0:T(8,128)(2,1)S(1)}, bf16[64,512]{1,0:T(8,128)(2,1)S(1)}, u32[]{:S(2)}, u32[]{:S(2)}) collective-permute-start(bf16[64,512]{1,0:T(8,128)(2,1)S(1)} %add_convert_fusion.1), channel_id=1, source_target_pairs={{0,16},{4,20},{8,24},{12,28},{16,0},{20,4},{24,8},{28,12},{1,17},{... | collective-permute-start | bytes 196616 | tf_op jit(solution)/shard_map/ppermute | solution.py:38
  21.3 3.2 %collective-permute-done.5 = bf16[64,512]{1,0:T(8,128)(2,1)S(1)} collective-permute-done((bf16[64,512]{1,0:T(8,128)(2,1)S(1)}, bf16[64,512]{1,0:T(8,128)(2,1)S(1)}, u32[]{:S(2)}, u32[]{:S(2)}) %collective-permute-start.5) | collective-permute-done | bytes 65568 | tf_op jit(solution)/shard_map/ppermute | solution.py:38
  24.5 0.6 %collective-permute-start.8 = (bf16[64,512]{1,0:T(8,128)(2,1)S(1)}, bf16[64,512]{1,0:T(8,128)(2,1)S(1)}, u32[]{:S(2)}, u32[]{:S(2)}) collective-permute-start(bf16[64,512]{1,0:T(8,128)(2,1)S(1)} %add_convert_fusion.rest_0_), channel_id=1, source_target_pairs={{0,12},{4,8},{8,4},{12,0},{16,28},{20,24},{24,20},{28,16},{1,13},{... | collective-permute-start | bytes 196616 | tf_op jit(solution)/shard_map/ppermute | solution.py:32
  25.1 1.6 %collective-permute-start.7 = (bf16[64,512]{1,0:T(8,128)(2,1)S(1)}, bf16[64,512]{1,0:T(8,128)(2,1)S(1)}, u32[]{:S(2)}, u32[]{:S(2)}) collective-permute-start(bf16[64,512]{1,0:T(8,128)(2,1)S(1)} %add_convert_fusion.rest_0_), channel_id=1, source_target_pairs={{0,8},{4,12},{8,0},{12,4},{16,24},{20,28},{24,16},{28,20},{1,9},{5... | collective-permute-start | bytes 196616 | tf_op jit(solution)/shard_map/ppermute | solution.py:32
  26.7 1.4 %collective-permute-start.6 = (bf16[64,512]{1,0:T(8,128)(2,1)S(1)}, bf16[64,512]{1,0:T(8,128)(2,1)S(1)}, u32[]{:S(2)}, u32[]{:S(2)}) collective-permute-start(bf16[64,512]{1,0:T(8,128)(2,1)S(1)} %add_convert_fusion.rest_0_), channel_id=1, source_target_pairs={{0,4},{4,0},{8,12},{12,8},{16,20},{20,16},{24,28},{28,24},{1,5},{5... | collective-permute-start | bytes 196616 | tf_op jit(solution)/shard_map/ppermute | solution.py:32
  28.1 1.7 %collective-permute-done.8.rest_3_ = bf16[64,512]{1,0:T(8,128)(2,1)S(1)} collective-permute-done((bf16[64,512]{1,0:T(8,128)(2,1)S(1)}, bf16[64,512]{1,0:T(8,128)(2,1)S(1)}, u32[]{:S(2)}, u32[]{:S(2)}) %collective-permute-start.8) | collective-permute-done | bytes 65568 | tf_op jit(solution)/shard_map/ppermute | solution.py:32
  29.8 1.2 %collective-permute-done.6.rest_1_ = bf16[64,512]{1,0:T(8,128)(2,1)S(1)} collective-permute-done((bf16[64,512]{1,0:T(8,128)(2,1)S(1)}, bf16[64,512]{1,0:T(8,128)(2,1)S(1)}, u32[]{:S(2)}, u32[]{:S(2)}) %collective-permute-start.6) | collective-permute-done | bytes 65568 | tf_op jit(solution)/shard_map/ppermute | solution.py:32
  31.0 0.9 %shard_map.68 = f32[1024,128]{1,0:T(8,128)} custom-call(f32[256,512]{1,0:T(8,128)S(1)} %get-tuple-element.19.base_ref, bf16[64,512]{1,0:T(8,128)(2,1)S(1)} %add_convert_fusion.rest_0_, bf16[64,512]{1,0:T(8,128)(2,1)S(1)} %collective-permute-done.6.rest_1_, bf16[64,512]{1,0:T(8,128)(2,1)S(1)} %collective-permute-done.7.rest_2_, ...), custom_call_target="tpu_custom_call" | custom-call | flops 524288 | bytes 1048576 | tf_op jit(solution)/shard_map/pallas_call | solution.py:262
  (14 shorter events, 0.1 us)
Async XLA Ops:
  0.7 1.0 %copy-start = (f32[2,128,4,128]{3,2,1,0:T(4,128)S(1)}, f32[2,128,4,128]{3,2,1,0:T(4,128)}, u32[]{:S(2)}) copy-start(f32[2,128,4,128]{3,2,1,0:T(4,128)} %param.7) | copy-start | bytes 1572868
  1.7 3.2 %copy-start.5 = (s32[128]{0:T(128)S(1)}, s32[128]{0:T(128)}, u32[]{:S(2)}) copy-start(s32[128]{0:T(128)} %param.10) | copy-start | bytes 1540
  1.7 3.3 %copy-start.1 = (f32[2,128,4,128]{3,2,1,0:T(4,128)S(1)}, f32[2,128,4,128]{3,2,1,0:T(4,128)}, u32[]{:S(2)}) copy-start(f32[2,128,4,128]{3,2,1,0:T(4,128)} %param.7) | copy-start | bytes 1572868
  1.7 3.3 %copy-start.4 = (f32[128,128]{1,0:T(8,128)S(1)}, f32[128,128]{1,0:T(8,128)}, u32[]{:S(2)}) copy-start(f32[128,128]{1,0:T(8,128)} %hamiltonian_ref.1) | copy-start | bytes 196612
  1.8 3.2 %copy-start.3 = (f32[128,128]{1,0:T(8,128)S(1)}, f32[128,128]{1,0:T(8,128)}, u32[]{:S(2)}) copy-start(f32[128,128]{1,0:T(8,128)} %coupling_ref.1) | copy-start | bytes 196612
  1.8 6.6 %collective-permute-start = (bf16[512,128]{1,0:T(8,128)(2,1)S(1)}, bf16[512,128]{1,0:T(8,128)(2,1)S(1)}, u32[]{:S(2)}, u32[]{:S(2)}) collective-permute-start(bf16[512,128]{1,0:T(8,128)(2,1)S(1)} %shard_map.64.mine_ref), channel_id=1, source_target_pairs={{0,2},{1,3},{2,0},{3,1},{4,6},{5,7},{6,4},{7,5},{8,10},{9,11},{10,... | collective-permute-start | bytes 393224 | tf_op jit(solution)/shard_map/ppermute | solution.py:220
  5.0 1.0 %copy-start.2 = (bf16[2,2,128,4,128]{4,3,2,1,0:T(4,128)(2,1)S(1)}, bf16[2,2,128,4,128]{4,3,2,1,0:T(4,128)(2,1)}, u32[]{:S(2)}) copy-start(bf16[2,2,128,4,128]{4,3,2,1,0:T(4,128)(2,1)} %param.6) | copy-start | bytes 1572868
  8.4 1.4 %collective-permute-start.1 = (bf16[512,128]{1,0:T(8,128)(2,1)S(1)}, bf16[512,128]{1,0:T(8,128)(2,1)S(1)}, u32[]{:S(2)}, u32[]{:S(2)}) collective-permute-start(bf16[512,128]{1,0:T(8,128)(2,1)S(1)} %shard_map.66.mine_ref), channel_id=1, source_target_pairs={{0,1},{1,0},{2,3},{3,2},{4,5},{5,4},{6,7},{7,6},{8,9},{9,8},{10,11... | collective-permute-start | bytes 393224 | tf_op jit(solution)/shard_map/ppermute | solution.py:220
  10.1 4.3 %collective-permute-start.2 = (bf16[64,512]{1,0:T(8,128)(2,1)S(1)}, bf16[64,512]{1,0:T(8,128)(2,1)S(1)}, u32[]{:S(2)}, u32[]{:S(2)}) collective-permute-start(bf16[64,512]{1,0:T(8,128)(2,1)S(1)} %get-tuple-element.24), channel_id=1, source_target_pairs={{0,4},{4,0},{8,12},{12,8},{16,20},{20,16},{24,28},{28,24},{1,5},{5... | collective-permute-start | bytes 196616 | tf_op jit(solution)/shard_map/ppermute | solution.py:32
  11.9 4.8 %collective-permute-start.3 = (bf16[64,512]{1,0:T(8,128)(2,1)S(1)}, bf16[64,512]{1,0:T(8,128)(2,1)S(1)}, u32[]{:S(2)}, u32[]{:S(2)}) collective-permute-start(bf16[64,512]{1,0:T(8,128)(2,1)S(1)} %get-tuple-element.25), channel_id=1, source_target_pairs={{0,8},{4,12},{8,0},{12,4},{16,24},{20,28},{24,16},{28,20},{1,9},{5... | collective-permute-start | bytes 196616 | tf_op jit(solution)/shard_map/ppermute | solution.py:32
  13.5 5.2 %collective-permute-start.4 = (bf16[64,512]{1,0:T(8,128)(2,1)S(1)}, bf16[64,512]{1,0:T(8,128)(2,1)S(1)}, u32[]{:S(2)}, u32[]{:S(2)}) collective-permute-start(bf16[64,512]{1,0:T(8,128)(2,1)S(1)} %get-tuple-element.26), channel_id=1, source_target_pairs={{0,12},{4,8},{8,4},{12,0},{16,28},{20,24},{24,20},{28,16},{1,13},{... | collective-permute-start | bytes 196616 | tf_op jit(solution)/shard_map/ppermute | solution.py:32
  18.7 5.8 %collective-permute-start.5 = (bf16[64,512]{1,0:T(8,128)(2,1)S(1)}, bf16[64,512]{1,0:T(8,128)(2,1)S(1)}, u32[]{:S(2)}, u32[]{:S(2)}) collective-permute-start(bf16[64,512]{1,0:T(8,128)(2,1)S(1)} %add_convert_fusion.1), channel_id=1, source_target_pairs={{0,16},{4,20},{8,24},{12,28},{16,0},{20,4},{24,8},{28,12},{1,17},{... | collective-permute-start | bytes 196616 | tf_op jit(solution)/shard_map/ppermute | solution.py:38
  24.5 5.2 %collective-permute-start.8 = (bf16[64,512]{1,0:T(8,128)(2,1)S(1)}, bf16[64,512]{1,0:T(8,128)(2,1)S(1)}, u32[]{:S(2)}, u32[]{:S(2)}) collective-permute-start(bf16[64,512]{1,0:T(8,128)(2,1)S(1)} %add_convert_fusion.rest_0_), channel_id=1, source_target_pairs={{0,12},{4,8},{8,4},{12,0},{16,28},{20,24},{24,20},{28,16},{1,13},{... | collective-permute-start | bytes 196616 | tf_op jit(solution)/shard_map/ppermute | solution.py:32
  25.1 4.7 %collective-permute-start.7 = (bf16[64,512]{1,0:T(8,128)(2,1)S(1)}, bf16[64,512]{1,0:T(8,128)(2,1)S(1)}, u32[]{:S(2)}, u32[]{:S(2)}) collective-permute-start(bf16[64,512]{1,0:T(8,128)(2,1)S(1)} %add_convert_fusion.rest_0_), channel_id=1, source_target_pairs={{0,8},{4,12},{8,0},{12,4},{16,24},{20,28},{24,16},{28,20},{1,9},{5... | collective-permute-start | bytes 196616 | tf_op jit(solution)/shard_map/ppermute | solution.py:32
  26.7 4.3 %collective-permute-start.6 = (bf16[64,512]{1,0:T(8,128)(2,1)S(1)}, bf16[64,512]{1,0:T(8,128)(2,1)S(1)}, u32[]{:S(2)}, u32[]{:S(2)}) collective-permute-start(bf16[64,512]{1,0:T(8,128)(2,1)S(1)} %add_convert_fusion.rest_0_), channel_id=1, source_target_pairs={{0,4},{4,0},{8,12},{12,8},{16,20},{20,16},{24,28},{28,24},{1,5},{5... | collective-permute-start | bytes 196616 | tf_op jit(solution)/shard_map/ppermute | solution.py:32
